TPU v7x, 32 devices: a whole 2x2x4 slice. The times are simulated.
32 devices in a mesh: dp: 8 (over y, x, core), mp: 4 (over z).
Axes of the slice: x: 2, y: 2, z: 4, core: 2. Of those that a mesh axis runs over, the one named last changes fastest.
Arguments:
- hidden_states: bfloat16 [4096, 4096], P('dp', 'mp'), may hold values from -40 to 40
- norm_gain: float32 [1, 4096], replicated, may hold values from 0.1 to 1.9
- query_weight: bfloat16 [1, 4096, 4096], P(None, 'dp', 'mp'), may hold values from -0.01171875 to 0.01171875
- keyvalue_weight: bfloat16 [1, 4096, 2, 4096], P(None, 'dp', None, 'mp'), may hold values from -0.09375 to 0.09375
- output_weight: bfloat16 [1, 4096, 4096], P(None, 'dp', 'mp'), may hold values from -0.09375 to 0.09375
- position_bias: float32 [1, 32, 64], P(None, None, 'mp'), may hold values from -8 to 250
- lengths: int32 [32], P('dp'), may hold values from 16 to 128
Outputs:
- layer_output: bfloat16 [4096, 4096], P('dp', 'mp')
All inputs are finite; a program needn't handle non-finite values.
Results may differ from a plain program's by a relative error of at most 0.006.
Values may be sent and summed in bfloat16 or wider, within the bound.
No kernel may reach another device: no remote copies, remote signals or barrier semaphores. Data moves between devices by JAX's collectives and lax.ppermute only.
A program may use at most 128 MiB of HBM per device.

v0:
```python
import jax
import jax.numpy as jnp
import numpy as np
from jax import lax
from jax.sharding import PartitionSpec as P

DH = 64
BUCKETS = 32
DIST = 128
LEN = 128


epsilon = 1e-06


def bucket_table():
    half_count = BUCKETS // 2
    exact_count = half_count // 2
    positions = np.arange(LEN)
    relative = positions[None, :] - positions[:, None]
    distance = np.abs(relative)
    scaled = (
        np.log(np.maximum(distance, 1) / exact_count)
        / np.log(DIST / exact_count)
        * (half_count - exact_count)
    )
    far_bucket = np.minimum(exact_count + np.floor(scaled + 1e-09).astype(np.int32), half_count - 1)
    near_bucket = np.where(distance < exact_count, distance, far_bucket)
    return (near_bucket + np.where(relative > 0, half_count, 0)).astype(np.int32)


def normed_rows(hidden, gain_row):
    values = hidden.astype(jnp.float32)
    mean_square = jnp.mean(values * values, axis=-1, keepdims=True)
    return (values * lax.rsqrt(mean_square + epsilon) * gain_row).astype(jnp.bfloat16)


def add_projections(query_acc, pair_acc, normed, query_piece, pair_piece):
    query_acc = jnp.dot(normed, query_piece, preferred_element_type=jnp.float32)
    pair_acc = jnp.einsum("td,dcf->ctf", normed, pair_piece, preferred_element_type=jnp.float32)
    return (query_acc, pair_acc)


def local(
    hidden_states, norm_gain, query_weight, keyvalue_weight, output_weight, position_bias, lengths
):
    captions = lengths.shape[0]
    tokens_here = hidden_states.shape[0]
    heads_here = position_bias.shape[2]
    inner_here = heads_here * DH
    bucket_onehot = jnp.asarray(
        (bucket_table()[:, :, None] == np.arange(BUCKETS)[None, None, :]).astype(np.float32)
    )
    visible = jnp.arange(LEN)[None, :] < lengths[:, None]
    hidden = hidden_states
    gathered = lax.all_gather(hidden, "mp", axis=1, tiled=True)
    normed = normed_rows(gathered, norm_gain[0])
    zero_queries = jnp.zeros((tokens_here, inner_here), jnp.float32)
    zero_pairs = jnp.zeros((2, tokens_here, inner_here), jnp.float32)
    query_rows = query_weight[0]
    pair_rows = keyvalue_weight[0]
    out_rows = output_weight[0]
    query_acc, pair_acc = add_projections(
        zero_queries,
        zero_pairs,
        normed,
        lax.all_gather(query_rows, "dp", axis=0, tiled=True),
        lax.all_gather(pair_rows, "dp", axis=0, tiled=True),
    )
    queries = query_acc.astype(jnp.bfloat16).reshape(captions, LEN, heads_here, DH)
    key_rows = pair_acc[0].astype(jnp.bfloat16).reshape(captions, LEN, heads_here, DH)
    value_rows = pair_acc[1].astype(jnp.bfloat16).reshape(captions, LEN, heads_here, DH)
    position_terms = jnp.einsum(
        "qkb,bh->hqk", bucket_onehot, position_bias[0], precision=lax.Precision.HIGHEST
    )
    scores = (
        jnp.einsum("cqhe,ckhe->chqk", queries, key_rows, preferred_element_type=jnp.float32)
        + position_terms[None]
    )
    scores = jnp.where(visible[:, None, None, :], scores, -1e30)
    maxima = jnp.max(scores, axis=-1, keepdims=True)
    raised = jnp.exp(scores - maxima)
    weights = (raised / jnp.sum(raised, axis=-1, keepdims=True)).astype(jnp.bfloat16)
    mixture = jnp.einsum("chqk,ckhe->cqhe", weights, value_rows, preferred_element_type=jnp.float32)
    attended = mixture.astype(jnp.bfloat16).reshape(tokens_here, inner_here)
    partial_out = jnp.einsum(
        "tf,df->td",
        attended,
        lax.all_gather(out_rows, "dp", axis=0, tiled=True),
        preferred_element_type=jnp.float32,
    )
    reduced = lax.psum_scatter(
        partial_out.astype(jnp.bfloat16), "mp", scatter_dimension=1, tiled=True
    ).astype(jnp.float32)
    hidden = (hidden.astype(jnp.float32) + reduced).astype(jnp.bfloat16)
    return hidden


def solution(mesh):
    in_specs = (
        P("dp", "mp"),
        P(),
        P(None, "dp", "mp"),
        P(None, "dp", None, "mp"),
        P(None, "dp", "mp"),
        P(None, None, "mp"),
        P("dp"),
    )
    out_specs = P("dp", "mp")
    return jax.shard_map(local, mesh=mesh, in_specs=in_specs, out_specs=out_specs, check_vma=False)
```

profile of v0, /device:TPU:0, one launch (start us, length us, event | category | flops | bytes accessed | tf_op | source)
XLA Modules:
  0.0 390.5 jit_solution(6013965719425897973)
XLA Ops:
  6.5 0.7 all-gather.8.cloned.1.call-update
  7.3 0.7 all-gather.12.cloned.1.call-update
  8.1 3.5 copy.15
  11.7 0.5 all-gather.14.cloned.1.call-update
  12.3 1.2 convolution_bitcast_fusion
  13.5 1.4 copy.21
  15.0 77.4 %all-gather.8.cloned.1.call-done = bf16[512,4096]{1,0:T(8,128)(2,1)} async-done(((bf16[512,1024]{1,0:T(8,128)(2,1)}), bf16[512,4096]{1,0:T(8,128)(2,1)}) %all-gather.8.cloned.1.call-update) | async-done | bytes 4194320 | tf_op jit(solution)/shard_map/all_gather | solution.py:56
  92.4 3.1 fusion.3
  95.5 51.6 %all-gather.12.cloned.1.call-done = bf16[1,4096,1024]{2,1,0:T(8,128)(2,1)} async-done(((bf16[1,512,1024]{2,1,0:T(8,128)(2,1)}), bf16[1,4096,1024]{2,1,0:T(8,128)(2,1)}) %all-gather.12.cloned.1.call-update) | async-done | bytes 8388624 | tf_op jit(solution)/shard_map/all_gather | solution.py:67
  147.1 9.2 %fusion.27 = bf16[512,1024]{1,0:T(8,128)(2,1)S(1)} fusion(bf16[1,4096,1024]{2,1,0:T(8,128)(2,1)} %all-gather.12.cloned.1.call-done, bf16[512,4096]{1,0:T(8,128)(2,1)} %all-gather.8.cloned.1.call-done, f32[4096]{0:T(1024)S(1)} %bitcast.40, f32[512]{0:T(512)S(1)} %add_rsqrt_fusion), kind=kOutput, calls=%fused_computation.28 | convolution fusion | flops 4303880192 | bytes 13649920 | tf_op jit(solution)/shard_map/dot_general | solution.py:39
  156.3 1.5 reshape.48
  157.8 80.9 %all-gather.10.cloned.1.call-done = bf16[1,4096,2,1024]{3,1,2,0:T(8,128)(2,1)} async-done(((bf16[1,512,2,1024]{3,1,2,0:T(8,128)(2,1)}), bf16[1,4096,2,1024]{3,1,2,0:T(8,128)(2,1)}) %all-gather.10.cloned.1.call-update) | async-done | bytes 16777232 | tf_op jit(solution)/shard_map/all_gather | solution.py:68
  238.7 13.7 %convert_bitcast_fusion = bf16[2,512,1024]{2,1,0:T(8,128)(2,1)S(1)} fusion(bf16[1,4096,2,1024]{3,1,2,0:T(8,128)(2,1)} %all-gather.10.cloned.1.call-done, bf16[512,4096]{1,0:T(8,128)(2,1)} %all-gather.8.cloned.1.call-done, f32[4096]{0:T(1024)S(1)} %bitcast.41, f32[512]{0:T(512)S(1)} %add_rsqrt_fusion), kind=kOutput, calls=%fused_computation.23 | convolution fusion | flops 8599371776 | bytes 23087104 | tf_op jit(solution)/shard_map/td,dcf->ctf/dot_general | solution.py:40
  252.4 1.1 fusion.42
  253.6 4.0 %reshape.49 = bf16[4,128,16,64]{3,2,1,0:T(8,128)(2,1)} reshape(bf16[1,512,1024]{2,1,0:T(8,128)(2,1)} %get-tuple-element.6) | data formatting | bytes 2097152 | tf_op jit(solution)/shard_map/convert_element_type | solution.py:71
  257.6 2.3 reshape.47
  259.9 3.3 fusion.15
  263.2 1.8 fusion.43
  265.0 0.8 fusion.33
  265.8 0.9 copy.24
  266.7 28.1 %all-gather.14.cloned.1.call-done = bf16[1,4096,1024]{2,1,0:T(8,128)(2,1)} async-done(((bf16[1,512,1024]{2,1,0:T(8,128)(2,1)}), bf16[1,4096,1024]{2,1,0:T(8,128)(2,1)}) %all-gather.14.cloned.1.call-update) | async-done | bytes 8388624 | tf_op jit(solution)/shard_map/all_gather | solution.py:89
  294.8 9.6 %fusion.10 = bf16[512,4096]{1,0:T(8,128)(2,1)} fusion(bf16[1,4096,1024]{2,1,0:T(8,128)(2,1)} %all-gather.14.cloned.1.call-done, bf16[128,8,4,128]{3,2,1,0:T(4,128)(2,1)S(1)} %bitcast.39), kind=kOutput, calls=%fused_computation.12 | convolution fusion | flops 4297064448 | bytes 13631488 | tf_op jit(solution)/shard_map/tf,df->td/dot_general | solution.py:86
  304.4 77.0 %reduce-scatter.2.cloned.1.call-done = bf16[512,1024]{1,0:T(8,128)(2,1)} async-done(((bf16[512,4096]{1,0:T(8,128)(2,1)}), bf16[512,1024]{1,0:T(8,128)(2,1)}) %reduce-scatter.2.cloned.1.call-update) | async-done | bytes 1048592 | tf_op jit(solution)/shard_map/reduce_scatter | solution.py:92
  381.3 2.6 add_convert_fusion
  (25 shorter events, 0.3 us)
Async XLA Ops:
  6.5 5.7 %copy-start = (f32[1,32,16]{1,2,0:T(8,128)S(1)}, f32[1,32,16]{1,2,0:T(8,128)}, u32[]{:S(2)}) copy-start(f32[1,32,16]{1,2,0:T(8,128)} %param.13) | copy-start | bytes 6148
  6.5 85.9 %all-gather.8.cloned.1.call-start = ((), (), s32[]{:S(2)}) async-start(), calls=%async_computation.1 | async-start | bytes 5242880 | tf_op jit(solution)/shard_map/all_gather | solution.py:56
  7.3 5.0 %copy-start.3 = (f32[128,128,32]{1,2,0:T(8,128)S(1)}, f32[128,128,32]{1,2,0:T(8,128)}, u32[]{:S(2)}) copy-start(f32[128,128,32]{1,2,0:T(8,128)} %constant.13.clone) | copy-start | bytes 6291460
  7.3 139.8 %all-gather.12.cloned.1.call-start = ((), (), s32[]{:S(2)}) async-start(), calls=%async_computation.4 | async-start | bytes 9437184 | tf_op jit(solution)/shard_map/all_gather | solution.py:67
  8.0 230.7 %all-gather.10.cloned.1.call-start = ((), (), s32[]{:S(2)}) async-start(), calls=%async_computation.3 | async-start | bytes 18874368 | tf_op jit(solution)/shard_map/all_gather | solution.py:68
  11.6 3.3 copy-start.7
  11.6 283.2 %all-gather.14.cloned.1.call-start = ((), (), s32[]{:S(2)}) async-start(), calls=%async_computation.5 | async-start | bytes 9437184 | tf_op jit(solution)/shard_map/all_gather | solution.py:89
  12.2 134.9 %copy-start.6 = (f32[1,4096]{1,0:T(1,128)S(1)}, f32[1,4096]{1,0:T(1,128)}, u32[]{:S(2)}) copy-start(f32[1,4096]{1,0:T(1,128)} %param.9) | copy-start | bytes 49156
  12.2 369.1 %reduce-scatter.2.cloned.1.call-start = ((), (), s32[]{:S(2)}) async-start(), calls=%async_computation.2 | async-start | bytes 5242880 | tf_op jit(solution)/shard_map/reduce_scatter | solution.py:92
  259.9 3.3 copy-start.5
  263.2 1.8 copy-start.4
  294.8 89.2 %copy-start.1 = (f32[1,32,16]{1,2,0:T(8,128)S(1)}, f32[1,32,16]{1,2,0:T(8,128)}, u32[]{:S(2)}) copy-start(f32[1,32,16]{1,2,0:T(8,128)} %param.13) | copy-start | bytes 6148
  304.4 77.0 %copy-start.2 = (bf16[512,1024]{1,0:T(8,128)(2,1)S(1)}, bf16[512,1024]{1,0:T(8,128)(2,1)}, u32[]{:S(2)}) copy-start(bf16[512,1024]{1,0:T(8,128)(2,1)} %param.8) | copy-start | bytes 3145732
Sparse Core Ops, SparseCore 0:
  8.9 83.4 all-gather.7
  94.3 52.7 all-gather.11
  149.0 89.7 all-gather.9
  240.5 54.2 all-gather.13
  304.5 76.7 reduce-scatter.1
where the time goes:
time: 391 us; the launch traced here: 390 us
  waiting for transfers between devices  317 us (81%)
  matrix products  37.7 us (10%)
  local copies, waits for them, and re-layouts  14.9 us (4%)
  between operations  13.2 us (3%)
  other arithmetic  7.56 us (2%)
    all_gather x1, waiting for transfers between devices, local(): lax.all_gather(pair_rows, 'dp', axis=0, tiled=True)  80.9 us
    all_gather x1, waiting for transfers between devices, local(): gathered = lax.all_gather(hidden, 'mp', axis=1, tiled=True)  77.4 us
    reduce_scatter x1, waiting for transfers between devices, local(): lax.psum_scatter(partial_out.astype(jnp.bfloat16), 'mp', scatter_dimensio...  77 us
    all_gather x1, waiting for transfers between devices, local(): lax.all_gather(query_rows, 'dp', axis=0, tiled=True)  51.6 us
    all_gather x1, waiting for transfers between devices, local(): lax.all_gather(out_rows, 'dp', axis=0, tiled=True)  28.1 us
    dot_general x1, matrix products, add_projections(): jnp.einsum('td,dcf->ctf', normed, pair_piece, preferred_element_type=jnp....  13.7 us
    dot_general x1, matrix products, local(): jnp.einsum('tf,df->td', attended, lax.all_gather(out_rows, 'dp', axis=0,...  9.59 us
    dot_general x1, matrix products, add_projections(): query_acc = jnp.dot(normed, query_piece, preferred_element_type=jnp.float32)  9.19 us
  transfers between devices with their start and end apart: 5, of which 5 were waited for; matrix products, arithmetic and copies ran while one was open for 12% of the time, Pallas kernels for 0%

commit v1 on v0

v1 whole, which is shorter than its diff:
```python
import functools

import jax
import jax.numpy as jnp
import numpy as np
from jax import lax
from jax.experimental import pallas as pl
from jax.experimental.pallas import tpu as pltpu
from jax.sharding import PartitionSpec as P

DH = 64
BUCKETS = 32
DIST = 128
LEN = 128
LANES = 128

epsilon = 1e-06

ANY = pl.BlockSpec(memory_space=pl.ANY)
SMEM = pl.BlockSpec(memory_space=pltpu.SMEM)
VMEM = pl.BlockSpec(memory_space=pltpu.VMEM)


def bucket_table():
    half_count = BUCKETS // 2
    exact_count = half_count // 2
    positions = np.arange(LEN)
    relative = positions[None, :] - positions[:, None]
    distance = np.abs(relative)
    scaled = (
        np.log(np.maximum(distance, 1) / exact_count)
        / np.log(DIST / exact_count)
        * (half_count - exact_count)
    )
    far_bucket = np.minimum(exact_count + np.floor(scaled + 1e-09).astype(np.int32), half_count - 1)
    near_bucket = np.where(distance < exact_count, distance, far_bucket)
    return (near_bucket + np.where(relative > 0, half_count, 0)).astype(np.int32)


def low_bit(p):
    return p & -p


def high_bit(p):
    return 1 << (p.bit_length() - 1)


def is_power(p):
    return p & (p - 1) == 0


def norm_kernel(groups, parts, *refs):
    xs = refs[: groups * parts]
    gain_ref, out_ref = refs[groups * parts :]
    features = parts * xs[0].shape[1]
    for u in range(groups):
        total = None
        for t in range(parts):
            x = xs[u * parts + t][...].astype(jnp.float32)
            s = jnp.sum(x * x, axis=-1, keepdims=True)
            total = s if total is None else total + s
        scale = lax.rsqrt(total * (1.0 / features) + epsilon)
        for t in range(parts):
            x = xs[u * parts + t][...].astype(jnp.float32)
            out_ref[t, u] = (x * scale * gain_ref[t][None, :]).astype(jnp.bfloat16)


def norm_call(pieces, gain_parts):
    groups, parts = len(pieces), len(pieces[0])
    rows, f = pieces[0][0].shape
    step = min(rows, 128)
    flat = [pieces[u][t] for u in range(groups) for t in range(parts)]
    return pl.pallas_call(
        functools.partial(norm_kernel, groups, parts),
        grid=(rows // step,),
        in_specs=[pl.BlockSpec((step, f), lambda i: (i, 0))] * len(flat)
        + [pl.BlockSpec((parts, f), lambda i: (0, 0))],
        out_specs=pl.BlockSpec((parts, groups, step, f), lambda i: (0, 0, i, 0)),
        out_shape=jax.ShapeDtypeStruct((parts, groups, rows, f), jnp.bfloat16),
        compiler_params=pltpu.CompilerParams(vmem_limit_bytes=48 * 2**20),
        cost_estimate=pl.CostEstimate(
            flops=8 * groups * parts * rows * f,
            bytes_accessed=4 * groups * parts * rows * f,
            transcendentals=0,
        ),
        name="norm",
    )(*flat, gain_parts)


def heads_kernel(planes, groups, tpos, cpos, lens, x_ref, *refs):
    w_refs = refs[: planes * groups]
    terms_ref, out_ref, xbuf, wbuf, acc, qkv, sems_x, sems_w = refs[planes * groups :]
    rows_w = w_refs[0].shape[1]
    n = w_refs[0].shape[2]
    tokens = xbuf.shape[1]
    per = tokens // groups
    heads = n // DH

    def x_copies(p):
        return [
            pltpu.make_async_copy(
                x_ref.at[tpos[p], u], xbuf.at[p, pl.ds(u * per, per)], sems_x.at[p, u]
            )
            for u in range(groups)
        ]

    def w_copies(p):
        return [
            pltpu.make_async_copy(
                w_refs[p * groups + u],
                wbuf.at[p, :, pl.ds(pl.multiple_of(cpos[u] * rows_w, rows_w), rows_w)],
                sems_w.at[p, u],
            )
            for u in range(groups)
        ]

    for p in range(planes):
        for c in x_copies(p) + w_copies(p):
            c.start()

    block = min(tokens, 256)
    for p in range(planes):
        for c in x_copies(p) + w_copies(p):
            c.wait()

        @pl.loop(0, tokens // block)
        def _(i):
            rows = pl.ds(pl.multiple_of(i * block, block), block)
            x = xbuf[p, rows, :]
            for m in range(3):
                part = jnp.dot(x, wbuf[p, m], preferred_element_type=jnp.float32)
                if p > 0:
                    part = acc[m, rows, :] + part
                if p < planes - 1:
                    acc[m, rows, :] = part
                else:
                    qkv[m, rows, :] = part.astype(jnp.bfloat16)

    lane_head = lax.broadcasted_iota(jnp.int32, (LEN, n), 1) // DH
    key_pos = lax.broadcasted_iota(jnp.int32, (LEN, LEN), 1)

    @pl.loop(0, tokens // LEN)
    def _(i):
        rows = pl.ds(pl.multiple_of(i * LEN, LEN), LEN)
        q = qkv[0, rows, :]
        k = qkv[1, rows, :]
        v = qkv[2, rows, :]
        zero = jnp.zeros_like(k)
        live = key_pos < lens[i]
        total = None
        for h in range(heads):
            own = lane_head == h
            s = lax.dot_general(
                q, jnp.where(own, k, zero), (((1,), (1,)), ((), ())),
                preferred_element_type=jnp.float32,
            )
            s = jnp.where(live, s + terms_ref[h], -1e30)
            e = jnp.exp(s - jnp.max(s, axis=-1, keepdims=True))
            w = (e / jnp.sum(e, axis=-1, keepdims=True)).astype(jnp.bfloat16)
            o = jnp.dot(w, jnp.where(own, v, zero), preferred_element_type=jnp.float32)
            total = o if total is None else total + o
        out_ref[rows, :] = total.astype(jnp.bfloat16)


def heads_call(planes, groups, tpos, cpos, lens, normed, weights, terms):
    _, rows_w, n = weights[0].shape
    _, _, per, f = normed.shape
    tokens = groups * per
    return pl.pallas_call(
        functools.partial(heads_kernel, planes, groups),
        in_specs=[SMEM, SMEM, SMEM, ANY] + [ANY] * len(weights) + [VMEM],
        out_specs=VMEM,
        out_shape=jax.ShapeDtypeStruct((tokens, n), jnp.bfloat16),
        scratch_shapes=[
            pltpu.VMEM((planes, tokens, f), jnp.bfloat16),
            pltpu.VMEM((planes, 3, f, n), jnp.bfloat16),
            pltpu.VMEM((3, tokens, n), jnp.float32),
            pltpu.VMEM((3, tokens, n), jnp.bfloat16),
            pltpu.SemaphoreType.DMA((planes, groups)),
            pltpu.SemaphoreType.DMA((planes, groups)),
        ],
        compiler_params=pltpu.CompilerParams(vmem_limit_bytes=56 * 2**20),
        cost_estimate=pl.CostEstimate(
            flops=2 * tokens * planes * f * 3 * n,
            bytes_accessed=2 * planes * f * (tokens + 3 * n),
            transcendentals=tokens * LEN * n // DH,
        ),
        name="heads",
    )(tpos, cpos, lens, normed, *weights, terms)


def project_kernel(planes, groups, column, last, ppos, qpos, cpos, *refs):
    count = planes * groups
    a_refs, w_refs, refs = refs[:count], refs[count : 2 * count], refs[2 * count :]
    if last:
        add_ref, res_ref, out_ref, abuf, wbuf, total, sems_a, sems_w = refs
    else:
        out_ref, abuf, wbuf, total, sems_a, sems_w = refs
    _, part_rows, inner = w_refs[0].shape
    nc = a_refs[0].shape[1]
    per_group = inner // groups

    def copies(t):
        out = []
        for u in range(groups):
            spot = pl.multiple_of(cpos[u] * nc, nc)
            out.append(
                pltpu.make_async_copy(
                    a_refs[t * groups + u], abuf.at[t, :, pl.ds(spot, nc)], sems_a.at[t, u]
                )
            )
            for p in range(planes):
                row = pl.multiple_of((cpos[u] * planes + qpos[p]) * part_rows, part_rows)
                for c in range(groups):
                    out.append(
                        pltpu.make_async_copy(
                            w_refs[p * groups + u].at[
                                ppos[t * planes + p], :, pl.ds(c * per_group + column, nc)
                            ],
                            wbuf.at[t, pl.ds(row, part_rows), pl.ds(c * nc, nc)],
                            sems_w.at[t, p, u, c],
                        )
                    )
        return out

    for t in range(planes):
        for copy in copies(t):
            copy.start()

    rows = out_ref.shape[0]
    block = min(rows, 128)
    for t in range(planes):
        for copy in copies(t):
            copy.wait()

        @pl.loop(0, rows // block)
        def _(i):
            here = pl.ds(pl.multiple_of(i * block, block), block)
            part = lax.dot_general(
                abuf[t, here, :],
                wbuf[t],
                (((1,), (1,)), ((), ())),
                preferred_element_type=jnp.float32,
            )
            if t > 0:
                part = part + total[here, :]
            elif last:
                part = part + add_ref[here, :]
            if t < planes - 1:
                total[here, :] = part
            elif last:
                residual = res_ref[here, :].astype(jnp.float32)
                out_ref[here, :] = (residual + part).astype(jnp.bfloat16)
            else:
                out_ref[here, :] = part


def project_call(planes, groups, column, places, attended, weights, before=None, residual=None):
    last = residual is not None
    rows, nc = attended[0].shape
    _, part_rows, _ = weights[0].shape
    width = planes * groups * part_rows
    ends = [before, residual] if last else []
    return pl.pallas_call(
        functools.partial(project_kernel, planes, groups, column, last),
        in_specs=[SMEM] * 3 + [ANY] * (2 * planes * groups) + [VMEM] * len(ends),
        out_specs=VMEM,
        out_shape=jax.ShapeDtypeStruct((rows, width), jnp.bfloat16 if last else jnp.float32),
        scratch_shapes=[
            pltpu.VMEM((planes, rows, groups * nc), jnp.bfloat16),
            pltpu.VMEM((planes, width, groups * nc), jnp.bfloat16),
            pltpu.VMEM((rows, width), jnp.float32),
            pltpu.SemaphoreType.DMA((planes, groups)),
            pltpu.SemaphoreType.DMA((planes, planes, groups, groups)),
        ],
        compiler_params=pltpu.CompilerParams(vmem_limit_bytes=40 * 2**20),
        cost_estimate=pl.CostEstimate(
            flops=2 * rows * width * planes * groups * nc,
            bytes_accessed=2 * planes * groups * nc * (rows + width),
            transcendentals=0,
        ),
        name="project",
    )(*places, *attended, *weights, *ends)


def after(value, *others):
    return lax.optimization_barrier((value,) + others)[0]


def local(
    dp_size, mp_size, hidden, norm_gain, query_weight, keyvalue_weight, output_weight, position_bias, lengths
):
    planes = mp_size
    groups = dp_size // mp_size
    tokens, f = hidden.shape
    inner_here = query_weight.shape[2]
    n = inner_here // groups
    chunks = 2 if n // 2 % LANES == 0 else 1
    nc = n // chunks
    heads = nc // DH
    rows_w = query_weight.shape[1]
    device = lax.axis_index("dp")
    z = lax.axis_index("mp")
    k, c = device // groups, device % groups

    def dp_xor(x, m):
        return lax.ppermute(x, "dp", [(i, i ^ m) for i in range(dp_size)])

    def mp_xor(x, m):
        return lax.ppermute(x, "mp", [(i, i ^ m) for i in range(mp_size)])

    def over_mp(x):
        got = [x]
        for t in range(1, planes):
            source = x if is_power(t) else got[t ^ low_bit(t)]
            got.append(mp_xor(source, t if is_power(t) else low_bit(t)))
        return got

    p_range = jnp.arange(planes, dtype=jnp.int32)
    cpos = (c ^ jnp.arange(groups, dtype=jnp.int32)).astype(jnp.int32)
    tpos = (z ^ k ^ p_range).astype(jnp.int32)
    qpos = (k ^ p_range).astype(jnp.int32)
    ppos = (z ^ k ^ p_range[:, None] ^ p_range[None, :]).astype(jnp.int32).reshape(-1)

    with jax.named_scope("hidden"):
        pieces = over_mp(hidden)
        rows_of = [pieces]
        for u in range(1, groups):
            rows_of.append([dp_xor(piece, u) for piece in pieces])
    gain_parts = norm_gain[0].reshape(planes, f)[z ^ p_range]

    def payload(u, chunk):
        start = (c ^ u) * n + chunk * nc
        q = lax.dynamic_slice(query_weight[0], (0, start), (rows_w, nc))
        kv = lax.dynamic_slice(keyvalue_weight[0], (0, 0, start), (rows_w, 2, nc))
        return jnp.stack([q, kv[:, 0], kv[:, 1]])

    chunk_weights = []
    tie = ()
    for chunk in range(chunks):
        with jax.named_scope("weights%d" % chunk):
            got = {}
            for u in range(groups):
                own = after(payload(u, chunk), *tie)
                for p in range(planes):
                    if p == 0:
                        got[p, u] = own if u == 0 else dp_xor(own, u)
                    elif is_power(p):
                        got[p, u] = dp_xor(own, p * groups ^ u)
            tie = tuple(got[p, u] for u in range(groups) for p in range(1, planes) if is_power(p))
            for u in range(groups):
                for p in range(1, planes):
                    if not is_power(p):
                        b = low_bit(p) if u % 2 == 0 else high_bit(p)
                        got[p, u] = dp_xor(got[p ^ b, u], b * groups)
            chunk_weights.append([got[p, u] for p in range(planes) for u in range(groups)])

    with jax.named_scope("turn"):
        part = rows_w // planes
        source = after(output_weight[0], *pieces[1:])
        moved = []
        for p in range(planes):
            block = lax.dynamic_slice(source, ((z ^ p) * part, 0), (part, inner_here))
            pairs = []
            for kk in range(planes):
                for cc in range(groups):
                    for zz in range(planes):
                        target = (zz ^ p) * groups + cc
                        pairs.append(((kk * groups + cc) * mp_size + zz, target * mp_size + kk))
            moved.append(lax.ppermute(block, ("dp", "mp"), pairs))
        turned = jnp.stack(moved)
    with jax.named_scope("output_weights"):
        turned = after(turned, *tie)
        out_got = {(0, 0): turned}
        for p in range(1, planes):
            if is_power(p):
                out_got[p, 0] = dp_xor(turned, p * groups)
        middle = planes // 2
        for p in range(1, planes):
            if not is_power(p):
                lo = dp_xor(out_got[p ^ low_bit(p), 0][:middle], low_bit(p) * groups)
                hi = dp_xor(out_got[p ^ high_bit(p), 0][middle:], high_bit(p) * groups)
                out_got[p, 0] = jnp.concatenate([lo, hi])
        for u in range(1, groups):
            for p in range(planes):
                out_got[p, u] = dp_xor(out_got[p, 0], u)
        out_weights = [out_got[p, u] for p in range(planes) for u in range(groups)]

    bucket_onehot = jnp.asarray(
        (bucket_table()[:, :, None] == np.arange(BUCKETS)[None, None, :]).astype(np.float32)
    )
    own_bias = lax.dynamic_slice(
        position_bias[0], (0, c * (n // DH)), (BUCKETS, n // DH)
    )
    terms = jnp.einsum("qkb,bh->hqk", bucket_onehot, own_bias, precision=lax.Precision.HIGHEST)
    lens = jnp.concatenate([lengths] + [dp_xor(lengths, u) for u in range(1, groups)])

    normed = norm_call(rows_of, gain_parts)

    total = None
    for chunk in range(chunks):
        attended = heads_call(
            planes,
            groups,
            tpos,
            cpos,
            lens,
            normed,
            chunk_weights[chunk],
            terms[chunk * heads : (chunk + 1) * heads],
        )
        with jax.named_scope("attended%d" % chunk):
            blocks = []
            for u in range(groups):
                block = attended[u * tokens : (u + 1) * tokens]
                blocks.append(over_mp(block if u == 0 else dp_xor(block, u)))
        flat = [blocks[u][t] for t in range(planes) for u in range(groups)]
        if chunk < chunks - 1:
            ends = {}
            assert chunks == 2
        else:
            ends = {"before": total, "residual": hidden}
            if total is None:
                ends["before"] = jnp.zeros((tokens, f), jnp.float32)
        total = project_call(
            planes, groups, chunk * nc, (ppos, qpos, cpos), flat, out_weights, **ends
        )
    return total


def solution(mesh):
    in_specs = (
        P("dp", "mp"),
        P(),
        P(None, "dp", "mp"),
        P(None, "dp", None, "mp"),
        P(None, "dp", "mp"),
        P(None, None, "mp"),
        P("dp"),
    )
    out_specs = P("dp", "mp")
    body = functools.partial(local, mesh.shape["dp"], mesh.shape["mp"])
    return jax.shard_map(body, mesh=mesh, in_specs=in_specs, out_specs=out_specs, check_vma=False)
```

time: 391 us -> 347 us (0.89)
  waiting for transfers between devices: 317 us -> 186 us
  Pallas kernels: 0 us -> 66.2 us
  starting transfers between devices: 0.16 us -> 55.1 us
  matrix products: 37.7 us -> 2.69 us
  local copies, waits for them, and re-layouts: 14.9 us -> 28.9 us
  between operations: 13.2 us -> 0.68 us
    all_gather x4 -> x0, waiting for transfers between devices: 238 us -> none  [the longest x1 80.9 us: local(): lax.all_gather(pair_rows, 'dp', axis=0, tiled=True)]
    ppermute x0 -> x48, waiting for transfers between devices: none -> 186 us  [the longest x15 97.3 us: mp_xor(): return lax.ppermute(x, 'mp', [(i, i ^ m) for i in range(mp_size)])]
    reduce_scatter x1 -> x0, waiting for transfers between devices: 77 us -> none  [local(): lax.psum_scatter(partial_out.astype(jnp.bfloat16), 'mp', scatter_dimensio...]
    pallas_call x0 -> x5, Pallas kernels: none -> 66.2 us  [the longest x2 37.7 us: heads_call(): pl.pallas_call(functools.partial(heads_kernel, planes, groups), in_specs=...]
    ppermute x0 -> x48, starting transfers between devices: none -> 55.1 us  [the longest x29 25.6 us: dp_xor(): return lax.ppermute(x, 'dp', [(i, i ^ m) for i in range(dp_size)])]
    dot_general x6 -> x1, matrix products: 37.7 us -> 2.69 us  [local(): jnp.einsum('qkb,bh->hqk', bucket_onehot, own_bias, precision=lax.Precisio...]
    unnamed x17 -> x90, local copies, waits for them, and re-layouts: 3.56 us -> 19.5 us
    convert_element_type x3 -> x0, local copies, waits for them, and re-layouts: 7.22 us -> none  [the longest x1 4.01 us: local(): pair_acc[0].astype(jnp.bfloat16).reshape(captions, LEN, heads_here, DH)]
  transfers between devices with their start and end apart: 5 -> 48, of which waited for: 5 -> 19; matrix products, arithmetic and copies ran while one was open for 12% -> 6% of each run, Pallas kernels for 0% -> 16%
where the time goes in v1:
time: 347 us; the launch traced here: 346 us
  waiting for transfers between devices  186 us (54%)
  Pallas kernels  66.2 us (19%)
  starting transfers between devices  55.1 us (16%)
  local copies, waits for them, and re-layouts  28.9 us (8%)
  other arithmetic  6.77 us (2%)
    ppermute x15, waiting for transfers between devices, mp_xor(): return lax.ppermute(x, 'mp', [(i, i ^ m) for i in range(mp_size)])  97.3 us
    ppermute x29, waiting for transfers between devices, dp_xor(): return lax.ppermute(x, 'dp', [(i, i ^ m) for i in range(dp_size)])  54.1 us
    pallas_call x2, Pallas kernels, heads_call(): pl.pallas_call(functools.partial(heads_kernel, planes, groups), in_specs=...  37.7 us
    ppermute x4, waiting for transfers between devices, local(): moved.append(lax.ppermute(block, ('dp', 'mp'), pairs))  34.3 us
    ppermute x29, starting transfers between devices, dp_xor(): return lax.ppermute(x, 'dp', [(i, i ^ m) for i in range(dp_size)])  25.6 us
    pallas_call x2, Pallas kernels, project_call(): pl.pallas_call(functools.partial(project_kernel, planes, groups, column,...  21.3 us
    ppermute x15, starting transfers between devices, mp_xor(): return lax.ppermute(x, 'mp', [(i, i ^ m) for i in range(mp_size)])  20.9 us
    unnamed x90, local copies, waits for them, and re-layouts  19.5 us
  transfers between devices with their start and end apart: 48, of which 19 were waited for; matrix products, arithmetic and copies ran while one was open for 6% of the time, Pallas kernels for 16%

profile of v1, /device:TPU:0, one launch (start us, length us, event | category | flops | bytes accessed | tf_op | source)
XLA Modules:
  0.0 346.0 jit_solution(266838636673675064)
XLA Ops:
  0.0 4.1 %collective-permute-start.2 = (bf16[512,1024]{1,0:T(8,128)(2,1)}, bf16[512,1024]{1,0:T(8,128)(2,1)S(1)}, u32[]{:S(2)}, u32[]{:S(2)}) collective-permute-start(bf16[512,1024]{1,0:T(8,128)(2,1)} %refs_17_.1), channel_id=1, source_target_pairs={{0,2},{1,3},{2,0},{3,1},{4,6},{5,7},{6,4},{7,5},{8,10},{9,11},{10,... | collective-permute-start | bytes 3145736 | tf_op jit(solution)/shard_map/hidden/ppermute | solution.py:310
  13.5 15.8 %collective-permute-done.11.refs_5_ = bf16[3,512,256]{2,1,0:T(8,128)(2,1)S(1)} collective-permute-done((bf16[3,512,256]{2,1,0:T(8,128)(2,1)}, bf16[3,512,256]{2,1,0:T(8,128)(2,1)S(1)}, u32[]{:S(2)}, u32[]{:S(2)}) %collective-permute-start.11) | collective-permute-done | bytes 786464 | tf_op jit(solution)/shard_map/weights0/ppermute | solution.py:307
  31.9 18.1 %collective-permute-done.2.refs_2_ = bf16[512,1024]{1,0:T(8,128)(2,1)S(1)} collective-permute-done((bf16[512,1024]{1,0:T(8,128)(2,1)}, bf16[512,1024]{1,0:T(8,128)(2,1)S(1)}, u32[]{:S(2)}, u32[]{:S(2)}) %collective-permute-start.2) | collective-permute-done | bytes 1048608 | tf_op jit(solution)/shard_map/hidden/ppermute | solution.py:310
  57.1 15.3 %collective-permute-done.1.refs_1_ = bf16[512,1024]{1,0:T(8,128)(2,1)S(1)} collective-permute-done((bf16[512,1024]{1,0:T(8,128)(2,1)S(1)}, bf16[512,1024]{1,0:T(8,128)(2,1)S(1)}, u32[]{:S(2)}, u32[]{:S(2)}) %collective-permute-start.1) | collective-permute-done | bytes 1048608 | tf_op jit(solution)/shard_map/hidden/ppermute | solution.py:310
  73.8 21.1 %collective-permute-done.3.refs_3_ = bf16[512,1024]{1,0:T(8,128)(2,1)S(1)} collective-permute-done((bf16[512,1024]{1,0:T(8,128)(2,1)S(1)}, bf16[512,1024]{1,0:T(8,128)(2,1)S(1)}, u32[]{:S(2)}, u32[]{:S(2)}) %collective-permute-start.3) | collective-permute-done | bytes 1048608 | tf_op jit(solution)/shard_map/hidden/ppermute | solution.py:310
  98.1 3.7 %collective-permute-start.26 = (bf16[128,1024]{1,0:T(8,128)(2,1)}, bf16[128,1024]{1,0:T(8,128)(2,1)}, u32[]{:S(2)}, u32[]{:S(2)}) collective-permute-start(bf16[128,1024]{1,0:T(8,128)(2,1)} %get-tuple-element.17), channel_id=1, source_target_pairs={{0,0},{1,8},{2,16},{3,24},{4,4},{5,12},{6,20},{7,28},{8,1},{9,9},{... | collective-permute-start | bytes 786440 | tf_op jit(solution)/shard_map/turn/ppermute | solution.py:370
  102.4 22.8 %collective-permute-done.14.refs_3_ = bf16[3,512,256]{2,1,0:T(8,128)(2,1)} collective-permute-done((bf16[3,512,256]{2,1,0:T(8,128)(2,1)}, bf16[3,512,256]{2,1,0:T(8,128)(2,1)}, u32[]{:S(2)}, u32[]{:S(2)}) %collective-permute-start.14) | collective-permute-done | bytes 786464 | tf_op jit(solution)/shard_map/weights1/ppermute | solution.py:307
  125.2 4.8 %collective-permute-start.28 = (bf16[128,1024]{1,0:T(8,128)(2,1)}, bf16[128,1024]{1,0:T(8,128)(2,1)S(1)}, u32[]{:S(2)}, u32[]{:S(2)}) collective-permute-start(bf16[128,1024]{1,0:T(8,128)(2,1)} %get-tuple-element.19), channel_id=1, source_target_pairs={{0,16},{1,24},{2,0},{3,8},{4,20},{5,28},{6,4},{7,12},{8,17},{9,25}... | collective-permute-start | bytes 786440 | tf_op jit(solution)/shard_map/turn/ppermute | solution.py:370
  132.7 3.9 %collective-permute-done.29 = bf16[128,1024]{1,0:T(8,128)(2,1)S(1)} collective-permute-done((bf16[128,1024]{1,0:T(8,128)(2,1)}, bf16[128,1024]{1,0:T(8,128)(2,1)S(1)}, u32[]{:S(2)}, u32[]{:S(2)}) %collective-permute-start.29) | collective-permute-done | bytes 262176 | tf_op jit(solution)/shard_map/turn/ppermute | solution.py:370
  136.6 21.3 %collective-permute-done.28 = bf16[128,1024]{1,0:T(8,128)(2,1)S(1)} collective-permute-done((bf16[128,1024]{1,0:T(8,128)(2,1)}, bf16[128,1024]{1,0:T(8,128)(2,1)S(1)}, u32[]{:S(2)}, u32[]{:S(2)}) %collective-permute-start.28) | collective-permute-done | bytes 262176 | tf_op jit(solution)/shard_map/turn/ppermute | solution.py:370
  158.0 10.1 %collective-permute-start.40 = (bf16[3,512,256]{2,1,0:T(8,128)(2,1)}, bf16[3,512,256]{2,1,0:T(8,128)(2,1)}, u32[]{:S(2)}, u32[]{:S(2)}) collective-permute-start(bf16[3,512,256]{2,1,0:T(8,128)(2,1)} %collective-permute-done.10.refs_3_), channel_id=1, source_target_pairs={{0,16},{4,20},{8,24},{12,28},{16,0},{20,4},{24,8},{28,12},{1,17},{... | collective-permute-start | bytes 2359304 | tf_op jit(solution)/shard_map/weights0/ppermute | solution.py:307
  168.1 9.1 %collective-permute-done.27 = bf16[128,1024]{1,0:T(8,128)(2,1)S(1)} collective-permute-done((bf16[128,1024]{1,0:T(8,128)(2,1)S(1)}, bf16[128,1024]{1,0:T(8,128)(2,1)S(1)}, u32[]{:S(2)}, u32[]{:S(2)}) %collective-permute-start.27) | collective-permute-done | bytes 262176 | tf_op jit(solution)/shard_map/turn/ppermute | solution.py:370
  189.5 7.2 %norm.1.x_ref = bf16[4,2,512,1024]{3,2,1,0:T(8,128)(2,1)} custom-call(bf16[512,1024]{1,0:T(8,128)(2,1)S(1)} %copy-done.3, bf16[512,1024]{1,0:T(8,128)(2,1)S(1)} %copy-done.13, bf16[512,1024]{1,0:T(8,128)(2,1)S(1)} %copy-done.9, bf16[512,1024]{1,0:T(8,128)(2,1)S(1)} %copy-done.15, bf16[512,1024]{1,0:T(8,128)(2,1)S(1)} %copy-done.11, ...), custom_call_target="tpu_custom_call" | custom-call | flops 33554432 | bytes 16777216 | tf_op jit(solution)/shard_map/norm/pallas_call | solution.py:73
  199.5 18.9 %heads.3 = bf16[1024,256]{1,0:T(8,128)(2,1)} custom-call(s32[4]{0:T(128)} %iota_xor_fusion.3.tpos, s32[2]{0:T(128)} %iota_xor_fusion.1.cpos, s32[8]{0:T(128)} %pad_add_fusion.lens, bf16[4,2,512,1024]{3,2,1,0:T(8,128)(2,1)} %norm.1.x_ref, bf16[3,512,256]{2,1,0:T(8,128)(2,1)} %copy-done.32, bf16[3,512,256]{2,1,0:T(8,128)(2,1)} %collective-permute-done.38.refs_1_, ...), custom_call_target="tpu_custom_call" | custom-call | flops 6442450944 | bytes 14680064 | tf_op jit(solution)/shard_map/heads/pallas_call | solution.py:169
  222.3 13.6 %collective-permute-done.17.refs_6_ = bf16[3,512,256]{2,1,0:T(8,128)(2,1)} collective-permute-done((bf16[3,512,256]{2,1,0:T(8,128)(2,1)}, bf16[3,512,256]{2,1,0:T(8,128)(2,1)}, u32[]{:S(2)}, u32[]{:S(2)}) %collective-permute-start.17) | collective-permute-done | bytes 786464 | tf_op jit(solution)/shard_map/weights1/ppermute | solution.py:307
  236.3 18.9 %heads.2 = bf16[1024,256]{1,0:T(8,128)(2,1)} custom-call(s32[4]{0:T(128)} %iota_xor_fusion.3.tpos, s32[2]{0:T(128)} %iota_xor_fusion.1.cpos, s32[8]{0:T(128)} %pad_add_fusion.lens, bf16[4,2,512,1024]{3,2,1,0:T(8,128)(2,1)} %norm.1.x_ref, bf16[3,512,256]{2,1,0:T(8,128)(2,1)} %pad_maximum_fusion.1.refs_0_, bf16[3,512,256]{2,1,0:T(8,128)(2,1)} %copy-done.41, ...), custom_call_target="tpu_custom_call" | custom-call | flops 6442450944 | bytes 14680064 | tf_op jit(solution)/shard_map/heads/pallas_call | solution.py:169
  257.3 6.8 %collective-permute-start.22 = (bf16[512,256]{1,0:T(8,128)(2,1)S(1)}, bf16[512,256]{1,0:T(8,128)(2,1)S(1)}, u32[]{:S(2)}, u32[]{:S(2)}) collective-permute-start(bf16[512,256]{1,0:T(8,128)(2,1)S(1)} %get-tuple-element.30.refs_0_), channel_id=1, source_target_pairs={{0,2},{1,3},{2,0},{3,1},{4,6},{5,7},{6,4},{7,5},{8,10},{9,11},{10,... | collective-permute-start | bytes 786440 | tf_op jit(solution)/shard_map/attended1/ppermute | solution.py:310
  265.7 10.7 %collective-permute-done.22.refs_4_ = bf16[512,256]{1,0:T(8,128)(2,1)S(1)} collective-permute-done((bf16[512,256]{1,0:T(8,128)(2,1)S(1)}, bf16[512,256]{1,0:T(8,128)(2,1)S(1)}, u32[]{:S(2)}, u32[]{:S(2)}) %collective-permute-start.22) | collective-permute-done | bytes 262176 | tf_op jit(solution)/shard_map/attended1/ppermute | solution.py:310
  280.4 10.4 %collective-permute-done.45.refs_5_ = bf16[512,256]{1,0:T(8,128)(2,1)} collective-permute-done((bf16[512,256]{1,0:T(8,128)(2,1)S(1)}, bf16[512,256]{1,0:T(8,128)(2,1)}, u32[]{:S(2)}, u32[]{:S(2)}) %collective-permute-start.45) | collective-permute-done | bytes 262176 | tf_op jit(solution)/shard_map/attended0/ppermute | solution.py:310
  293.9 8.9 %collective-permute-done.46.refs_6_ = bf16[512,256]{1,0:T(8,128)(2,1)S(1)} collective-permute-done((bf16[512,256]{1,0:T(8,128)(2,1)S(1)}, bf16[512,256]{1,0:T(8,128)(2,1)S(1)}, u32[]{:S(2)}, u32[]{:S(2)}) %collective-permute-start.46) | collective-permute-done | bytes 262176 | tf_op jit(solution)/shard_map/attended0/ppermute | solution.py:310
  303.7 3.1 collective-permute-done.23.refs_5_
  306.8 6.3 %collective-permute-done.47.refs_7_ = bf16[512,256]{1,0:T(8,128)(2,1)} collective-permute-done((bf16[512,256]{1,0:T(8,128)(2,1)}, bf16[512,256]{1,0:T(8,128)(2,1)}, u32[]{:S(2)}, u32[]{:S(2)}) %collective-permute-start.47) | collective-permute-done | bytes 262176 | tf_op jit(solution)/shard_map/attended0/ppermute | solution.py:310
  322.2 10.1 %project.2.refs_16_ = f32[512,1024]{1,0:T(8,128)S(1)} custom-call(s32[16]{0:T(128)S(1)} %xor.78.ppos, s32[4]{0:T(128)S(1)} %iota_xor_fusion.2.qpos, s32[2]{0:T(128)S(1)} %copy-done.30, bf16[512,256]{1,0:T(8,128)(2,1)S(1)} %copy-done.17, bf16[512,256]{1,0:T(8,128)(2,1)S(1)} %copy-done.21, bf16[512,256]{1,0:T(8,128)(2,1)S(1)} %copy-done.25, ...), custom_call_target="tpu_custom_call" | custom-call | flops 2147483648 | bytes 6291456 | tf_op jit(solution)/shard_map/project/pallas_call | solution.py:264
  334.7 11.2 %project.3 = bf16[512,1024]{1,0:T(8,128)(2,1)} custom-call(s32[16]{0:T(128)S(1)} %xor.78.ppos, s32[4]{0:T(128)S(1)} %iota_xor_fusion.2.qpos, s32[2]{0:T(128)S(1)} %copy-done.30, bf16[512,256]{1,0:T(8,128)(2,1)S(1)} %get-tuple-element.30.refs_0_, bf16[512,256]{1,0:T(8,128)(2,1)} %collective-permute-done.19.refs_1_, ...), custom_call_target="tpu_custom_call" | custom-call | flops 2147483648 | bytes 6291456 | tf_op jit(solution)/shard_map/project/pallas_call | solution.py:264
  (199 shorter events, 69.1 us)
Async XLA Ops:
  0.0 50.0 %collective-permute-start.2 = (bf16[512,1024]{1,0:T(8,128)(2,1)}, bf16[512,1024]{1,0:T(8,128)(2,1)S(1)}, u32[]{:S(2)}, u32[]{:S(2)}) collective-permute-start(bf16[512,1024]{1,0:T(8,128)(2,1)} %refs_17_.1), channel_id=1, source_target_pairs={{0,2},{1,3},{2,0},{3,1},{4,6},{5,7},{6,4},{7,5},{8,10},{9,11},{10,... | collective-permute-start | bytes 3145736 | tf_op jit(solution)/shard_map/hidden/ppermute | solution.py:310
  12.4 39.4 %collective-permute-start.9 = (bf16[3,512,256]{2,1,0:T(8,128)(2,1)S(1)}, bf16[3,512,256]{2,1,0:T(8,128)(2,1)}, u32[]{:S(2)}, u32[]{:S(2)}) collective-permute-start(bf16[3,512,256]{2,1,0:T(8,128)(2,1)S(1)} %pad_maximum_fusion.2.refs_0_), channel_id=1, source_target_pairs={{0,16},{4,20},{8,24},{12,28},{16,0},{20,4},{24,8},{28,12},{1,17},{... | collective-permute-start | bytes 2359304 | tf_op jit(solution)/shard_map/weights0/ppermute | solution.py:307
  13.0 38.9 %collective-permute-start.8 = (bf16[3,512,256]{2,1,0:T(8,128)(2,1)S(1)}, bf16[3,512,256]{2,1,0:T(8,128)(2,1)S(1)}, u32[]{:S(2)}, u32[]{:S(2)}) collective-permute-start(bf16[3,512,256]{2,1,0:T(8,128)(2,1)S(1)} %pad_maximum_fusion.2.refs_0_), channel_id=1, source_target_pairs={{0,8},{4,12},{8,0},{12,4},{16,24},{20,28},{24,16},{28,20},{1,9},{5... | collective-permute-start | bytes 2359304 | tf_op jit(solution)/shard_map/weights0/ppermute | solution.py:307
  30.3 42.0 %collective-permute-start.1 = (bf16[512,1024]{1,0:T(8,128)(2,1)S(1)}, bf16[512,1024]{1,0:T(8,128)(2,1)S(1)}, u32[]{:S(2)}, u32[]{:S(2)}) collective-permute-start(bf16[512,1024]{1,0:T(8,128)(2,1)S(1)} %copy-done.2), channel_id=1, source_target_pairs={{0,1},{1,0},{2,3},{3,2},{4,5},{5,4},{6,7},{7,6},{8,9},{9,8},{10,11... | collective-permute-start | bytes 3145736 | tf_op jit(solution)/shard_map/hidden/ppermute | solution.py:310
  50.0 44.8 %collective-permute-start.3 = (bf16[512,1024]{1,0:T(8,128)(2,1)S(1)}, bf16[512,1024]{1,0:T(8,128)(2,1)S(1)}, u32[]{:S(2)}, u32[]{:S(2)}) collective-permute-start(bf16[512,1024]{1,0:T(8,128)(2,1)S(1)} %collective-permute-done.2.refs_2_), channel_id=1, source_target_pairs={{0,1},{1,0},{2,3},{3,2},{4,5},{5,4},{6,7},{7,6},{8,9},{9,8},{10,11... | collective-permute-start | bytes 3145736 | tf_op jit(solution)/shard_map/hidden/ppermute | solution.py:310
  51.8 46.3 %collective-permute-start.15 = (bf16[3,512,256]{2,1,0:T(8,128)(2,1)}, bf16[3,512,256]{2,1,0:T(8,128)(2,1)}, u32[]{:S(2)}, u32[]{:S(2)}) collective-permute-start(bf16[3,512,256]{2,1,0:T(8,128)(2,1)} %pad_maximum_fusion.1.refs_0_), channel_id=1, source_target_pairs={{0,16},{4,20},{8,24},{12,28},{16,0},{20,4},{24,8},{28,12},{1,17},{... | collective-permute-start | bytes 2359304 | tf_op jit(solution)/shard_map/weights1/ppermute | solution.py:307
  53.4 71.8 %collective-permute-start.6 = (bf16[512,1024]{1,0:T(8,128)(2,1)S(1)}, bf16[512,1024]{1,0:T(8,128)(2,1)}, u32[]{:S(2)}, u32[]{:S(2)}) collective-permute-start(bf16[512,1024]{1,0:T(8,128)(2,1)S(1)} %collective-permute-done.2.refs_2_), channel_id=1, source_target_pairs={{0,4},{4,0},{8,12},{12,8},{16,20},{20,16},{24,28},{28,24},{1,5},{5... | collective-permute-start | bytes 3145736 | tf_op jit(solution)/shard_map/hidden/ppermute | solution.py:307
  55.6 46.3 %collective-permute-start.13 = (bf16[3,512,256]{2,1,0:T(8,128)(2,1)}, bf16[3,512,256]{2,1,0:T(8,128)(2,1)}, u32[]{:S(2)}, u32[]{:S(2)}) collective-permute-start(bf16[3,512,256]{2,1,0:T(8,128)(2,1)} %pad_maximum_fusion.1.refs_0_), channel_id=1, source_target_pairs={{0,8},{4,12},{8,0},{12,4},{16,24},{20,28},{24,16},{28,20},{1,9},{5... | collective-permute-start | bytes 2359304 | tf_op jit(solution)/shard_map/weights1/ppermute | solution.py:307
  101.9 81.4 %collective-permute-start.5 = (bf16[512,1024]{1,0:T(8,128)(2,1)S(1)}, bf16[512,1024]{1,0:T(8,128)(2,1)}, u32[]{:S(2)}, u32[]{:S(2)}) collective-permute-start(bf16[512,1024]{1,0:T(8,128)(2,1)S(1)} %collective-permute-done.1.refs_1_), channel_id=1, source_target_pairs={{0,4},{4,0},{8,12},{12,8},{16,20},{20,16},{24,28},{28,24},{1,5},{5... | collective-permute-start | bytes 3145736 | tf_op jit(solution)/shard_map/hidden/ppermute | solution.py:307
  102.3 81.0 %collective-permute-start.7 = (bf16[512,1024]{1,0:T(8,128)(2,1)S(1)}, bf16[512,1024]{1,0:T(8,128)(2,1)}, u32[]{:S(2)}, u32[]{:S(2)}) collective-permute-start(bf16[512,1024]{1,0:T(8,128)(2,1)S(1)} %collective-permute-done.3.refs_3_), channel_id=1, source_target_pairs={{0,4},{4,0},{8,12},{12,8},{16,20},{20,16},{24,28},{28,24},{1,5},{5... | collective-permute-start | bytes 3145736 | tf_op jit(solution)/shard_map/hidden/ppermute | solution.py:307
  125.2 32.7 %collective-permute-start.28 = (bf16[128,1024]{1,0:T(8,128)(2,1)}, bf16[128,1024]{1,0:T(8,128)(2,1)S(1)}, u32[]{:S(2)}, u32[]{:S(2)}) collective-permute-start(bf16[128,1024]{1,0:T(8,128)(2,1)} %get-tuple-element.19), channel_id=1, source_target_pairs={{0,16},{1,24},{2,0},{3,8},{4,20},{5,28},{6,4},{7,12},{8,17},{9,25}... | collective-permute-start | bytes 786440 | tf_op jit(solution)/shard_map/turn/ppermute | solution.py:370
  130.0 47.2 %collective-permute-start.27 = (bf16[128,1024]{1,0:T(8,128)(2,1)S(1)}, bf16[128,1024]{1,0:T(8,128)(2,1)S(1)}, u32[]{:S(2)}, u32[]{:S(2)}) collective-permute-start(bf16[128,1024]{1,0:T(8,128)(2,1)S(1)} %get-tuple-element.20), channel_id=1, source_target_pairs={{0,8},{1,0},{2,24},{3,16},{4,12},{5,4},{6,28},{7,20},{8,9},{9,1},{... | collective-permute-start | bytes 786440 | tf_op jit(solution)/shard_map/turn/ppermute | solution.py:370
  136.6 60.2 %collective-permute-start.38 = (bf16[3,512,256]{2,1,0:T(8,128)(2,1)}, bf16[3,512,256]{2,1,0:T(8,128)(2,1)}, u32[]{:S(2)}, u32[]{:S(2)}) collective-permute-start(bf16[3,512,256]{2,1,0:T(8,128)(2,1)} %pad_maximum_fusion.3), channel_id=1, source_target_pairs={{0,4},{4,0},{8,12},{12,8},{16,20},{20,16},{24,28},{28,24},{1,5},{5... | collective-permute-start | bytes 2359304 | tf_op jit(solution)/shard_map/weights0/ppermute | solution.py:307
  158.0 38.8 %collective-permute-start.40 = (bf16[3,512,256]{2,1,0:T(8,128)(2,1)}, bf16[3,512,256]{2,1,0:T(8,128)(2,1)}, u32[]{:S(2)}, u32[]{:S(2)}) collective-permute-start(bf16[3,512,256]{2,1,0:T(8,128)(2,1)} %collective-permute-done.10.refs_3_), channel_id=1, source_target_pairs={{0,16},{4,20},{8,24},{12,28},{16,0},{20,4},{24,8},{28,12},{1,17},{... | collective-permute-start | bytes 2359304 | tf_op jit(solution)/shard_map/weights0/ppermute | solution.py:307
  183.2 36.2 %collective-permute-start.33 = (bf16[4,128,1024]{2,1,0:T(8,128)(2,1)S(1)}, bf16[4,128,1024]{2,1,0:T(8,128)(2,1)S(1)}, u32[]{:S(2)}, u32[]{:S(2)}) collective-permute-start(bf16[4,128,1024]{2,1,0:T(8,128)(2,1)S(1)} %pad_maximum_fusion.refs_8_), channel_id=1, source_target_pairs={{0,16},{4,20},{8,24},{12,28},{16,0},{20,4},{24,8},{28,12},{1,17},{... | collective-permute-start | bytes 3145736 | tf_op jit(solution)/shard_map/output_weights/ppermute | solution.py:307
  183.3 37.0 %collective-permute-start.31 = (bf16[4,128,1024]{2,1,0:T(8,128)(2,1)S(1)}, bf16[4,128,1024]{2,1,0:T(8,128)(2,1)S(1)}, u32[]{:S(2)}, u32[]{:S(2)}) collective-permute-start(bf16[4,128,1024]{2,1,0:T(8,128)(2,1)S(1)} %pad_maximum_fusion.refs_8_), channel_id=1, source_target_pairs={{0,8},{4,12},{8,0},{12,4},{16,24},{20,28},{24,16},{28,20},{1,9},{5... | collective-permute-start | bytes 3145736 | tf_op jit(solution)/shard_map/output_weights/ppermute | solution.py:307
  196.8 39.2 %collective-permute-start.17 = (bf16[3,512,256]{2,1,0:T(8,128)(2,1)}, bf16[3,512,256]{2,1,0:T(8,128)(2,1)}, u32[]{:S(2)}, u32[]{:S(2)}) collective-permute-start(bf16[3,512,256]{2,1,0:T(8,128)(2,1)} %collective-permute-done.15.refs_4_), channel_id=1, source_target_pairs={{0,8},{4,12},{8,0},{12,4},{16,24},{20,28},{24,16},{28,20},{1,9},{5... | collective-permute-start | bytes 2359304 | tf_op jit(solution)/shard_map/weights1/ppermute | solution.py:307
  198.0 38.3 %collective-permute-start.18 = (bf16[3,512,256]{2,1,0:T(8,128)(2,1)}, bf16[3,512,256]{2,1,0:T(8,128)(2,1)}, u32[]{:S(2)}, u32[]{:S(2)}) collective-permute-start(bf16[3,512,256]{2,1,0:T(8,128)(2,1)} %collective-permute-done.14.refs_3_), channel_id=1, source_target_pairs={{0,16},{4,20},{8,24},{12,28},{16,0},{20,4},{24,8},{28,12},{1,17},{... | collective-permute-start | bytes 2359304 | tf_op jit(solution)/shard_map/weights1/ppermute | solution.py:307
  219.5 57.0 %collective-permute-start.30 = (bf16[4,128,1024]{2,1,0:T(8,128)(2,1)S(1)}, bf16[4,128,1024]{2,1,0:T(8,128)(2,1)S(1)}, u32[]{:S(2)}, u32[]{:S(2)}) collective-permute-start(bf16[4,128,1024]{2,1,0:T(8,128)(2,1)S(1)} %pad_maximum_fusion.refs_8_), channel_id=1, source_target_pairs={{0,4},{4,0},{8,12},{12,8},{16,20},{20,16},{24,28},{28,24},{1,5},{5... | collective-permute-start | bytes 3145736 | tf_op jit(solution)/shard_map/output_weights/ppermute | solution.py:307
  220.3 34.8 %collective-permute-start.41 = (bf16[512,256]{1,0:T(8,128)(2,1)S(1)}, bf16[512,256]{1,0:T(8,128)(2,1)S(1)}, u32[]{:S(2)}, u32[]{:S(2)}) collective-permute-start(bf16[512,256]{1,0:T(8,128)(2,1)S(1)} %get-tuple-element.25), channel_id=1, source_target_pairs={{0,4},{4,0},{8,12},{12,8},{16,20},{20,16},{24,28},{28,24},{1,5},{5... | collective-permute-start | bytes 786440 | tf_op jit(solution)/shard_map/attended0/ppermute | solution.py:307
  220.4 36.9 %collective-permute-start.44 = (bf16[512,256]{1,0:T(8,128)(2,1)S(1)}, bf16[512,256]{1,0:T(8,128)(2,1)S(1)}, u32[]{:S(2)}, u32[]{:S(2)}) collective-permute-start(bf16[512,256]{1,0:T(8,128)(2,1)S(1)} %get-tuple-element.26.refs_0_), channel_id=1, source_target_pairs={{0,2},{1,3},{2,0},{3,1},{4,6},{5,7},{6,4},{7,5},{8,10},{9,11},{10,... | collective-permute-start | bytes 786440 | tf_op jit(solution)/shard_map/attended0/ppermute | solution.py:310
  264.2 48.9 %collective-permute-start.34 = (bf16[4,128,1024]{2,1,0:T(8,128)(2,1)S(1)}, bf16[4,128,1024]{2,1,0:T(8,128)(2,1)}, u32[]{:S(2)}, u32[]{:S(2)}) collective-permute-start(bf16[4,128,1024]{2,1,0:T(8,128)(2,1)S(1)} %collective-permute-done.33.refs_12_), channel_id=1, source_target_pairs={{0,4},{4,0},{8,12},{12,8},{16,20},{20,16},{24,28},{28,24},{1,5},{5... | collective-permute-start | bytes 3145736 | tf_op jit(solution)/shard_map/output_weights/ppermute | solution.py:307
  264.4 50.7 %collective-permute-start.32 = (bf16[4,128,1024]{2,1,0:T(8,128)(2,1)S(1)}, bf16[4,128,1024]{2,1,0:T(8,128)(2,1)}, u32[]{:S(2)}, u32[]{:S(2)}) collective-permute-start(bf16[4,128,1024]{2,1,0:T(8,128)(2,1)S(1)} %collective-permute-done.31.refs_10_), channel_id=1, source_target_pairs={{0,4},{4,0},{8,12},{12,8},{16,20},{20,16},{24,28},{28,24},{1,5},{5... | collective-permute-start | bytes 3145736 | tf_op jit(solution)/shard_map/output_weights/ppermute | solution.py:307
  265.5 49.6 %collective-permute-start.37 = (bf16[4,128,1024]{2,1,0:T(8,128)(2,1)}, bf16[4,128,1024]{2,1,0:T(8,128)(2,1)}, u32[]{:S(2)}, u32[]{:S(2)}) collective-permute-start(bf16[4,128,1024]{2,1,0:T(8,128)(2,1)} %constant_dynamic-update-slice_fusion.refs_14_), channel_id=1, source_target_pairs={{0,4},{4,0},{8,12},{12,8},{16,20},{20,16},{24,28},{28,24},{1,5},{5... | collective-permute-start | bytes 3145736 | tf_op jit(solution)/shard_map/output_weights/ppermute | solution.py:307
  (67 other events, 1318.6 us)
